TPU v7x, 32 devices: a whole 2x2x4 slice. The times are simulated.
32 devices in a mesh: col: 2 (over x), row: 16 (over z, y, core).
Axes of the slice: x: 2, y: 2, z: 4, core: 2. Of those that a mesh axis runs over, the one named last changes fastest.
Arguments:
- residual: bfloat16 [1024, 2880], P('row'), may hold values from -6 to 6
- query_states: bfloat16 [1024, 4096], P('row', 'col'), may hold values from -48 to 48
- key_states: bfloat16 [1024, 512], P('row'), may hold values from -24 to 24
- value_states: bfloat16 [1024, 512], P('row'), may hold values from -6 to 6
- segment_ids: int32 [1024], P('row'), may hold values from 0 to 3, never falling along the last dimension, each value on 1 to 512 neighbouring positions
- sink_logits: float32 [64], P('col'), may hold values from -2 to 4
- w_out: bfloat16 [4096, 2880], P('col'), may hold values from -0.375 to 0.375
- norm_gain: float32 [2880], replicated, may hold values from 0.5 to 1.5
- expert_ids: int32 [1024, 4], P('row'), may hold values from 0 to 15, all different within a row; in each aligned block of 64 rows (0 to 63, 64 to 127, ...) at most 32 rows name the same one
- route_weight: float32 [1024, 4], P('row'), may hold values from 0.05 to 0.45
- w_gate_up: bfloat16 [16, 2, 2880, 2880], P('row', None, None, 'col'), may hold values from -0.109375 to 0.109375
- w_down: bfloat16 [16, 2880, 2880], P('row', 'col'), may hold values from -0.109375 to 0.109375
Outputs:
- layer_out: bfloat16 [1024, 2880], P('row', 'col')
Inputs may be any that keep to these rules, and one draw needn't show every extreme that they name: `expert_ids`: each token names 4 different experts; among the 64 tokens of one index of row no expert is named by more than 32 tokens, and in every draw some expert is named by exactly 32 of them. `segment_ids`: segment numbers never fall along the tokens.
All inputs are finite; a program needn't handle non-finite values.
Results may differ from a plain program's by a relative error of at most 0.018.
Values may be sent and summed in bfloat16 or wider, within the bound.
A program may use at most 128 MiB of HBM per device.

v0:
```python
import jax
import jax.numpy as jnp
from jax import lax
from jax.sharding import PartitionSpec as P

HEADS = 64
KV_HEADS = 8
HEAD_DIM = 64
WINDOW = 128
TOP = 4
epsilon = 1e-05
masked_score = -1e30


def shifted(shard, axis, by):
    size = lax.axis_size(axis)
    pairs = [(i, i + by) for i in range(size) if 0 <= i + by < size]
    return lax.ppermute(shard, axis, pairs)


def normalize(stream_rows, norm_gain):
    values32 = stream_rows.astype(jnp.float32)
    square_mean = jnp.mean(values32 * values32, axis=-1, keepdims=True)
    return (values32 * lax.rsqrt(square_mean + epsilon) * norm_gain).astype(jnp.bfloat16)


def attend(query_groups, key_groups, value_groups, allowed, sink_groups):
    scores = jnp.einsum(
        "tgjd,lgd->gjtl", query_groups, key_groups, preferred_element_type=jnp.float32
    )
    scores = scores * query_groups.shape[-1] ** (-0.5)
    scores = jnp.where(allowed[None, None], scores, masked_score)
    peak_score = jnp.maximum(jnp.max(scores, axis=-1, keepdims=True), sink_groups)
    numerator = jnp.exp(scores - peak_score)
    denominator = jnp.exp(sink_groups - peak_score) + jnp.sum(numerator, axis=-1, keepdims=True)
    weights = (numerator / denominator).astype(jnp.bfloat16)
    return jnp.einsum(
        "gjtl,lgd->tgjd", weights, value_groups, preferred_element_type=jnp.float32
    ).astype(jnp.bfloat16)


def local(
    residual,
    query_states,
    key_states,
    value_states,
    segment_ids,
    sink_logits,
    w_out,
    norm_gain,
    expert_ids,
    route_weight,
    w_gate_up,
    w_down,
):
    tok_rows = query_states.shape[0]
    row_count = lax.axis_size("row")
    col_count = lax.axis_size("col")
    row_index = lax.axis_index("row")
    col_index = lax.axis_index("col")
    local_heads = sink_logits.shape[0]
    group_size = HEADS // KV_HEADS
    if local_heads >= group_size:
        kv_count = local_heads // group_size
        kv_first = col_index * kv_count
    else:
        kv_count = 1
        kv_first = col_index * local_heads // group_size
    kv_width = kv_count * HEAD_DIM
    own_keys = lax.dynamic_slice_in_dim(key_states, kv_first * HEAD_DIM, kv_width, 1)
    own_values = lax.dynamic_slice_in_dim(value_states, kv_first * HEAD_DIM, kv_width, 1)
    shift_count = (WINDOW + tok_rows - 2) // tok_rows
    key_parts = []
    value_parts = []
    segment_parts = []
    start_parts = []
    for offset in range(shift_count, 0, -1):
        arrived = shifted((own_keys, own_values, segment_ids), "row", offset)
        key_parts.append(arrived[0])
        value_parts.append(arrived[1])
        segment_parts.append(arrived[2])
        start_parts.append((row_index - offset) * tok_rows)
    key_parts.append(own_keys)
    value_parts.append(own_values)
    segment_parts.append(segment_ids)
    start_parts.append(row_index * tok_rows)
    key_groups = jnp.concatenate(key_parts, 0).reshape(-1, kv_count, HEAD_DIM)
    value_groups = jnp.concatenate(value_parts, 0).reshape(-1, kv_count, HEAD_DIM)
    key_segments = jnp.concatenate(segment_parts, 0)
    positions = jnp.arange(tok_rows, dtype=jnp.int32)
    key_position = jnp.concatenate([start + positions for start in start_parts], 0)
    query_position = row_index * tok_rows + positions
    allowed = (key_position[None, :] >= 0) & (key_position[None, :] <= query_position[:, None])
    allowed = allowed & (key_position[None, :] > query_position[:, None] - WINDOW)
    allowed = allowed & (key_segments[None, :] == segment_ids[:, None])
    query_groups = query_states.reshape(tok_rows, kv_count, local_heads // kv_count, HEAD_DIM)
    sink_groups = sink_logits.reshape(kv_count, local_heads // kv_count, 1, 1)
    attended = attend(query_groups, key_groups, value_groups, allowed, sink_groups).reshape(
        tok_rows, local_heads * HEAD_DIM
    )
    partial_value = jnp.dot(attended, w_out, preferred_element_type=jnp.float32)
    feature_count = residual.shape[1] // col_count
    experts_all = w_gate_up.shape[0] * row_count
    slot_cap = max(2, 2 * TOP * tok_rows // experts_all)
    routing = jnp.concatenate([expert_ids.astype(jnp.float32), route_weight], 1)
    routing = lax.all_gather(routing, "row", axis=0, tiled=False)
    names_mine = routing[:, :, :TOP] == row_index.astype(jnp.float32)
    mine = jnp.any(names_mine, axis=2)
    weight = jnp.sum(jnp.where(names_mine, routing[:, :, TOP:], 0.0), axis=2)
    slot_of = jnp.cumsum(mine.astype(jnp.int32), axis=1) - 1
    slots = jnp.arange(slot_cap, dtype=jnp.int32)
    chosen = mine[:, None, :] & (slot_of[:, None, :] == slots[None, :, None])
    selector = chosen.astype(jnp.bfloat16)
    combine = jnp.where(chosen, weight[:, None, :], 0.0)
    expert_gate_up = w_gate_up[0]
    expert_down = w_down[0]
    summed = lax.psum(partial_value.astype(jnp.bfloat16), "col").astype(jnp.float32)
    stream = (residual.astype(jnp.float32) + summed).astype(jnp.bfloat16)
    stream_part = lax.dynamic_slice_in_dim(stream, col_index * feature_count, feature_count, 1)
    source_rows = normalize(stream, norm_gain)
    gathered = lax.all_gather(source_rows, "row", axis=0, tiled=False)
    packed = (
        jnp.einsum("nst,ntd->nsd", selector, gathered, preferred_element_type=jnp.float32)
        .astype(jnp.bfloat16)
        .reshape(row_count * slot_cap, -1)
    )
    gate = jnp.dot(packed, expert_gate_up[0], preferred_element_type=jnp.float32)
    up = jnp.dot(packed, expert_gate_up[1], preferred_element_type=jnp.float32)
    active = ((up + 1.0) * gate * jax.nn.sigmoid(1.702 * gate)).astype(jnp.bfloat16)
    expert_partial = jnp.dot(active, expert_down, preferred_element_type=jnp.float32)
    scaled = expert_partial.reshape(row_count, slot_cap, -1) * jnp.sum(combine, 2)[:, :, None]
    mixed = (
        jnp.einsum(
            "nst,nsd->ntd",
            selector,
            scaled.astype(jnp.bfloat16),
            preferred_element_type=jnp.float32,
        )
        .astype(jnp.bfloat16)
        .reshape(row_count * tok_rows, -1)
    )
    mixed = lax.psum_scatter(mixed, "row", scatter_dimension=0, tiled=True)
    mixed = lax.psum_scatter(mixed, "col", scatter_dimension=1, tiled=True)
    return (stream_part.astype(jnp.float32) + mixed.astype(jnp.float32)).astype(jnp.bfloat16)


def solution(mesh):
    in_specs = (
        P("row", None),
        P("row", "col"),
        P("row", None),
        P("row", None),
        P("row"),
        P("col"),
        P("col", None),
        P(),
        P("row", None),
        P("row", None),
        P("row", None, None, "col"),
        P("row", "col", None),
    )
    out_specs = P("row", "col")
    return jax.shard_map(local, mesh=mesh, in_specs=in_specs, out_specs=out_specs, check_vma=False)
```

profile of v0, /device:TPU:0, one launch (start us, length us, event | category | flops | bytes accessed | tf_op | source)
XLA Modules:
  0.0 268.6 jit_solution(8531859856784551742)
XLA Ops:
  6.5 2.5 collective-permute-start.3
  9.1 4.4 %collective-permute-start.2 = (s32[64]{0:T(128)}, s32[64]{0:T(128)S(1)}, u32[]{:S(2)}, u32[]{:S(2)}) collective-permute-start(s32[64]{0:T(128)} %param.16), channel_id=1, source_target_pairs={{0,2},{1,3},{2,4},{3,5},{4,6},{5,7},{6,8},{7,9},{8,10},{9,11},{10,... | collective-permute-start | bytes 776 | tf_op jit(solution)/shard_map/ppermute | solution.py:18
  13.5 3.2 %collective-permute-start.1 = (bf16[64,256]{1,0:T(8,128)(2,1)S(1)}, bf16[64,256]{1,0:T(8,128)(2,1)S(1)}, u32[]{:S(2)}, u32[]{:S(2)}) collective-permute-start(bf16[64,256]{1,0:T(8,128)(2,1)S(1)} %constant_dynamic-slice_fusion.1), channel_id=1, source_target_pairs={{0,1},{1,2},{2,3},{3,4},{4,5},{5,6},{6,7},{7,8},{8,9},{9,10},{10,1... | collective-permute-start | bytes 98312 | tf_op jit(solution)/shard_map/ppermute | solution.py:18
  16.8 3.4 %collective-permute-start = (bf16[64,256]{1,0:T(8,128)(2,1)S(1)}, bf16[64,256]{1,0:T(8,128)(2,1)S(1)}, u32[]{:S(2)}, u32[]{:S(2)}) collective-permute-start(bf16[64,256]{1,0:T(8,128)(2,1)S(1)} %constant_dynamic-slice_fusion.1), channel_id=1, source_target_pairs={{0,2},{1,3},{2,4},{3,5},{4,6},{5,7},{6,8},{7,9},{8,10},{9,11},{10,... | collective-permute-start | bytes 98312 | tf_op jit(solution)/shard_map/ppermute | solution.py:18
  21.0 1.9 collective-permute-start.5
  23.8 1.5 reshape.191
  25.2 3.4 %collective-permute-start.4 = (bf16[64,256]{1,0:T(8,128)(2,1)S(1)}, bf16[64,256]{1,0:T(8,128)(2,1)S(1)}, u32[]{:S(2)}, u32[]{:S(2)}) collective-permute-start(bf16[64,256]{1,0:T(8,128)(2,1)S(1)} %constant_dynamic-slice_fusion), channel_id=1, source_target_pairs={{0,2},{1,3},{2,4},{3,5},{4,6},{5,7},{6,8},{7,9},{8,10},{9,11},{10,... | collective-permute-start | bytes 98312 | tf_op jit(solution)/shard_map/ppermute | solution.py:18
  31.9 1.1 convolution_convert_fusion.3
  33.0 1.9 copy-done.1
  34.8 4.4 %convolution_convert_fusion.2 = bf16[64,2880]{1,0:T(8,128)(2,1)} fusion(bf16[64,2048]{0,1:T(8,128)(2,1)S(1)} %bitcast.59, bf16[2048,2880]{0,1:T(8,128)(2,1)S(1)} %copy-done.1), kind=kOutput, calls=%fused_computation.11 | convolution fusion | flops 755159040 | bytes 12427264 | tf_op jit(solution)/shard_map/dot_general | solution.py:101
  39.3 26.4 %all-reduce.2.cloned.1.call-done = bf16[64,2880]{1,0:T(8,128)(2,1)} async-done(((bf16[64,2880]{1,0:T(8,128)(2,1)}), bf16[64,2880]{1,0:T(8,128)(2,1)}) %all-reduce.2.cloned.1.call-update) | async-done | bytes 368656 | tf_op jit(solution)/shard_map/psum | solution.py:117
  65.7 1.2 fusion.23
  67.0 0.9 fusion.25
  68.0 22.1 %all-gather.2 = f32[16,64,8]{1,2,0:T(8,128)S(1)} all-gather(f32[1,64,8]{1,2,0:T(8,128)S(1)} %maximum_bitcast_fusion), channel_id=2, replica_groups=mesh['col'=2,'row'=16] {'row'}, dimensions={0}, use_global_device_ids=true | all-gather | bytes 34816 | tf_op jit(solution)/shard_map/all_gather | solution.py:106
  90.6 37.7 %all-gather.5.cloned.1.call-done = bf16[1024,2880]{1,0:T(8,128)(2,1)} async-done(((bf16[64,2880]{1,0:T(8,128)(2,1)}), bf16[1024,2880]{1,0:T(8,128)(2,1)}) %all-gather.5.cloned.1.call-update) | async-done | bytes 5898256 | tf_op jit(solution)/shard_map/all_gather | solution.py:121
  128.4 3.7 %convolution_convert_fusion.1 = bf16[16,32,2880]{2,1,0:T(8,128)(2,1)S(1)} fusion(bf16[16,64,2880]{2,1,0:T(8,128)(2,1)} %bitcast.54, s32[16,64]{1,0:T(8,128)S(1)} %broadcast_add_fusion, pred[16,64]{1,0:T(8,128)(4,1)S(1)} %reduce_or.9), kind=kOutput, calls=%fused_computation.10 | convolution fusion | flops 190283776 | bytes 8852480 | tf_op jit(solution)/shard_map/nst,ntd->nsd/dot_general | solution.py:123
  132.0 7.2 %fusion.2 = f32[512,1440]{0,1:T(8,128)S(1)} fusion(bf16[512,2880]{1,0:T(8,128)(2,1)S(1)} %bitcast.55, bf16[1,2,2880,1440]{2,3,1,0:T(8,128)(2,1)} %param.22), kind=kOutput, calls=%fused_computation.2 | convolution fusion | flops 4246732800 | bytes 14376960 | tf_op jit(solution)/shard_map/dot_general | solution.py:127
  139.2 8.8 %fusion.19 = bf16[512,1440]{0,1:T(8,128)(2,1)S(1)} fusion(f32[512,1440]{0,1:T(8,128)S(1)} %fusion.2, bf16[512,2880]{1,0:T(8,128)(2,1)S(1)} %bitcast.56, bf16[1,2,2880,1440]{2,3,1,0:T(8,128)(2,1)} %param.22), kind=kOutput, calls=%fused_computation.15 | convolution fusion | flops 4252631040 | bytes 15851520 | tf_op jit(solution)/shard_map/dot_general | solution.py:128
  148.8 10.8 %convolution_convert_fusion = bf16[16,64,2880]{2,1,0:T(8,128)(2,1)} fusion(bf16[16,32,1440]{2,1,0:T(8,128)(2,1)S(1)} %bitcast.58, bf16[1,1440,2880]{2,1,0:T(8,128)(2,1)} %param.23, f32[16,32]{1,0:T(8,128)S(1)} %select_reduce_fusion, s32[16,64]{1,0:T(8,128)S(1)} %broadcast_add_fusion, pred[16,64]{1,0:T(8,128)(4,1)S(1)} %reduce_or.9), kind=kOutput, calls=%fused_computation.9 | convolution fusion | flops 4441440256 | bytes 15674368 | tf_op jit(solution)/shard_map/nst,nsd->ntd/dot_general | solution.py:133
  159.6 82.0 %reduce-scatter.5.cloned.1.call-done = bf16[64,2880]{1,0:T(8,128)(2,1)} async-done(((bf16[1024,2880]{1,0:T(8,128)(2,1)}), bf16[64,2880]{1,0:T(8,128)(2,1)}) %reduce-scatter.5.cloned.1.call-update) | async-done | bytes 368656 | tf_op jit(solution)/shard_map/reduce_scatter | solution.py:142
  241.6 2.1 copy.26
  243.8 16.3 %reduce-scatter.7.cloned.1.call-done = bf16[1440,64]{1,0:T(8,128)(2,1)} async-done(((bf16[2880,64]{1,0:T(8,128)(2,1)}), bf16[1440,64]{1,0:T(8,128)(2,1)}) %reduce-scatter.7.cloned.1.call-update) | async-done | bytes 184336
  260.1 1.1 copy.27
  261.2 0.8 add_convert_fusion.1
  (51 shorter events, 6.1 us)
Async XLA Ops:
  6.5 7.0 %copy-start = (bf16[64,512]{1,0:T(8,128)(2,1)S(1)}, bf16[64,512]{1,0:T(8,128)(2,1)}, u32[]{:S(2)}) copy-start(bf16[64,512]{1,0:T(8,128)(2,1)} %param.15) | copy-start | bytes 196612
  6.5 59.2 %all-reduce.2.cloned.1.call-start = ((), (), s32[]{:S(2)}) async-start(), calls=%async_computation.2 | async-start | bytes 753664 | tf_op jit(solution)/shard_map/psum | solution.py:117
  6.5 18.7 %collective-permute-start.3 = (s32[64]{0:T(128)}, s32[64]{0:T(128)S(1)}, u32[]{:S(2)}, u32[]{:S(2)}) collective-permute-start(s32[64]{0:T(128)} %param.16), channel_id=1, source_target_pairs={{0,1},{1,2},{2,3},{3,4},{4,5},{5,6},{6,7},{7,8},{8,9},{9,10},{10,1... | collective-permute-start | bytes 776 | tf_op jit(solution)/shard_map/ppermute | solution.py:18
  9.1 19.6 %collective-permute-start.2 = (s32[64]{0:T(128)}, s32[64]{0:T(128)S(1)}, u32[]{:S(2)}, u32[]{:S(2)}) collective-permute-start(s32[64]{0:T(128)} %param.16), channel_id=1, source_target_pairs={{0,2},{1,3},{2,4},{3,5},{4,6},{5,7},{6,8},{7,9},{8,10},{9,11},{10,... | collective-permute-start | bytes 776 | tf_op jit(solution)/shard_map/ppermute | solution.py:18
  13.5 16.6 %collective-permute-start.1 = (bf16[64,256]{1,0:T(8,128)(2,1)S(1)}, bf16[64,256]{1,0:T(8,128)(2,1)S(1)}, u32[]{:S(2)}, u32[]{:S(2)}) collective-permute-start(bf16[64,256]{1,0:T(8,128)(2,1)S(1)} %constant_dynamic-slice_fusion.1), channel_id=1, source_target_pairs={{0,1},{1,2},{2,3},{3,4},{4,5},{5,6},{6,7},{7,8},{8,9},{9,10},{10,1... | collective-permute-start | bytes 98312 | tf_op jit(solution)/shard_map/ppermute | solution.py:18
  16.8 13.4 %collective-permute-start = (bf16[64,256]{1,0:T(8,128)(2,1)S(1)}, bf16[64,256]{1,0:T(8,128)(2,1)S(1)}, u32[]{:S(2)}, u32[]{:S(2)}) collective-permute-start(bf16[64,256]{1,0:T(8,128)(2,1)S(1)} %constant_dynamic-slice_fusion.1), channel_id=1, source_target_pairs={{0,2},{1,3},{2,4},{3,5},{4,6},{5,7},{6,8},{7,9},{8,10},{9,11},{10,... | collective-permute-start | bytes 98312 | tf_op jit(solution)/shard_map/ppermute | solution.py:18
  21.0 9.3 %collective-permute-start.5 = (bf16[64,256]{1,0:T(8,128)(2,1)S(1)}, bf16[64,256]{1,0:T(8,128)(2,1)S(1)}, u32[]{:S(2)}, u32[]{:S(2)}) collective-permute-start(bf16[64,256]{1,0:T(8,128)(2,1)S(1)} %constant_dynamic-slice_fusion), channel_id=1, source_target_pairs={{0,1},{1,2},{2,3},{3,4},{4,5},{5,6},{6,7},{7,8},{8,9},{9,10},{10,1... | collective-permute-start | bytes 98312 | tf_op jit(solution)/shard_map/ppermute | solution.py:18
  25.2 5.1 %collective-permute-start.4 = (bf16[64,256]{1,0:T(8,128)(2,1)S(1)}, bf16[64,256]{1,0:T(8,128)(2,1)S(1)}, u32[]{:S(2)}, u32[]{:S(2)}) collective-permute-start(bf16[64,256]{1,0:T(8,128)(2,1)S(1)} %constant_dynamic-slice_fusion), channel_id=1, source_target_pairs={{0,2},{1,3},{2,4},{3,5},{4,6},{5,7},{6,8},{7,9},{8,10},{9,11},{10,... | collective-permute-start | bytes 98312 | tf_op jit(solution)/shard_map/ppermute | solution.py:18
  30.5 4.4 %copy-start.1 = (bf16[2048,2880]{0,1:T(8,128)(2,1)S(1)}, bf16[2048,2880]{0,1:T(8,128)(2,1)}, u32[]{:S(2)}) copy-start(bf16[2048,2880]{0,1:T(8,128)(2,1)} %param.18) | copy-start | bytes 35389444
  34.8 30.9 %copy-start.2 = (bf16[64,2880]{1,0:T(8,128)(2,1)S(1)}, bf16[64,2880]{1,0:T(8,128)(2,1)}, u32[]{:S(2)}) copy-start(bf16[64,2880]{1,0:T(8,128)(2,1)} %param.12) | copy-start | bytes 1105924
  34.8 32.2 %copy-start.3 = (f32[2880]{0:T(1024)S(1)}, f32[2880]{0:T(1024)}, u32[]{:S(2)}) copy-start(f32[2880]{0:T(1024)} %param.19) | copy-start | bytes 34564
  34.8 33.2 %copy-start.4 = (s32[64,4]{0,1:T(4,128)S(1)}, s32[64,4]{0,1:T(4,128)}, u32[]{:S(2)}) copy-start(s32[64,4]{0,1:T(4,128)} %param.20) | copy-start | bytes 3076
  34.8 33.2 %copy-start.5 = (f32[64,4]{0,1:T(4,128)S(1)}, f32[64,4]{0,1:T(4,128)}, u32[]{:S(2)}) copy-start(f32[64,4]{0,1:T(4,128)} %param.21) | copy-start | bytes 3076
  39.3 89.1 %all-gather.5.cloned.1.call-start = ((), (), s32[]{:S(2)}) async-start(), calls=%async_computation.4 | async-start | bytes 6406144 | tf_op jit(solution)/shard_map/all_gather | solution.py:121
  67.9 173.7 %reduce-scatter.5.cloned.1.call-start = ((), (), s32[]{:S(2)}) async-start(), calls=%async_computation.3 | async-start | bytes 6406144 | tf_op jit(solution)/shard_map/reduce_scatter | solution.py:142
  159.6 100.5 %reduce-scatter.7.cloned.1.call-start = ((), (), s32[]{:S(2)}) async-start(), calls=%async_computation.5 | async-start | bytes 1105920
Sparse Core Ops, SparseCore 0:
  39.4 26.2 all-reduce.1
  68.0 60.2 all-gather.4
  159.7 81.8 reduce-scatter.4
  243.9 16.1 reduce-scatter.6
where the time goes:
time: 269 us
  waiting for transfers between devices  163 us (61%)
  matrix products  36.5 us (14%)
  blocking collectives  22.1 us (8%)
  starting transfers between devices  19.1 us (7%)
  between operations  13.4 us (5%)
  local copies, waits for them, and re-layouts  9.04 us (3%)
  other arithmetic  5.84 us (2%)
    reduce_scatter x1, waiting for transfers between devices, local(): mixed = lax.psum_scatter(mixed, 'row', scatter_dimension=0, tiled=True)  82 us
    all_gather x1, waiting for transfers between devices, local(): gathered = lax.all_gather(source_rows, 'row', axis=0, tiled=False)  37.7 us
    psum x1, waiting for transfers between devices, local(): lax.psum(partial_value.astype(jnp.bfloat16), 'col').astype(jnp.float32)  26.4 us
    all_gather x1, blocking collectives, local(): routing = lax.all_gather(routing, 'row', axis=0, tiled=False)  22.1 us
    ppermute x6, starting transfers between devices, shifted(): return lax.ppermute(shard, axis, pairs)  19 us
    unnamed x5, waiting for transfers between devices  16.4 us
    dot_general x1, matrix products, local(): jnp.einsum('nst,nsd->ntd', selector, scaled.astype(jnp.bfloat16), preferr...  10.8 us
    dot_general x1, matrix products, local(): up = jnp.dot(packed, expert_gate_up[1], preferred_element_type=jnp.float32)  8.82 us
  transfers between devices with their start and end apart: 10, of which 4 were waited for; matrix products, arithmetic and copies ran while one was open for 2% of the time, Pallas kernels for 0%

commit v1 on v0

--- a/solution.py
+++ b/solution.py
@@ -1,3 +1,4 @@
+import functools
 import jax
 import jax.numpy as jnp
 from jax import lax
@@ -10,6 +11,15 @@
 TOP = 4
 epsilon = 1e-05
 masked_score = -1e30
+
+
+def name_frame(q_in, device_axis):
+    tile_out = lax.all_gather(q_in, device_axis)
+    w1 = jnp.sum(tile_out, axis=0)
+    return w1
+
+
+fix_sections_here = functools.partial(name_frame, device_axis="col")
 
 
 def shifted(shard, axis, by):
@@ -114,7 +124,7 @@
     combine = jnp.where(chosen, weight[:, None, :], 0.0)
     expert_gate_up = w_gate_up[0]
     expert_down = w_down[0]
-    summed = lax.psum(partial_value.astype(jnp.bfloat16), "col").astype(jnp.float32)
+    summed = fix_sections_here(partial_value.astype(jnp.bfloat16)).astype(jnp.float32)
     stream = (residual.astype(jnp.float32) + summed).astype(jnp.bfloat16)
     stream_part = lax.dynamic_slice_in_dim(stream, col_index * feature_count, feature_count, 1)
     source_rows = normalize(stream, norm_gain)

time: 269 us -> 253 us (0.941)
  waiting for transfers between devices: 163 us -> 138 us
  blocking collectives: 22.1 us -> 32.3 us
    psum x1 -> x0, waiting for transfers between devices: 26.4 us -> none  [local(): lax.psum(partial_value.astype(jnp.bfloat16), 'col').astype(jnp.float32)]
    all_gather x0 -> x1, blocking collectives: none -> 12.1 us  [name_frame(): tile_out = lax.all_gather(q_in, device_axis)]
    unnamed x5 -> x4, waiting for transfers between devices: 16.4 us -> 16.4 us
  transfers between devices with their start and end apart: 10 -> 9, of which waited for: 4 -> 3; matrix products, arithmetic and copies ran while one was open for 2% -> 2% of each run, Pallas kernels for 0% -> 0%
where the time goes in v1:
time: 253 us
  waiting for transfers between devices  138 us (55%)
  matrix products  35.8 us (14%)
  blocking collectives  32.3 us (13%)
  starting transfers between devices  19 us (8%)
  between operations  13.5 us (5%)
  local copies, waits for them, and re-layouts  9.05 us (4%)
  other arithmetic  5.1 us (2%)
    reduce_scatter x1, waiting for transfers between devices, local(): mixed = lax.psum_scatter(mixed, 'row', scatter_dimension=0, tiled=True)  81.9 us
    all_gather x1, waiting for transfers between devices, local(): gathered = lax.all_gather(source_rows, 'row', axis=0, tiled=False)  39.4 us
    all_gather x1, blocking collectives, local(): routing = lax.all_gather(routing, 'row', axis=0, tiled=False)  20.2 us
    ppermute x6, starting transfers between devices, shifted(): return lax.ppermute(shard, axis, pairs)  19 us
    unnamed x4, waiting for transfers between devices  16.4 us
    all_gather x1, blocking collectives, name_frame(): tile_out = lax.all_gather(q_in, device_axis)  12.1 us
    dot_general x1, matrix products, local(): jnp.einsum('nst,nsd->ntd', selector, scaled.astype(jnp.bfloat16), preferr...  10.8 us
    dot_general x1, matrix products, local(): up = jnp.dot(packed, expert_gate_up[1], preferred_element_type=jnp.float32)  8.82 us
  transfers between devices with their start and end apart: 9, of which 3 were waited for; matrix products, arithmetic and copies ran while one was open for 2% of the time, Pallas kernels for 0%

profile of v1, /device:TPU:0, one launch (start us, length us, event | category | flops | bytes accessed | tf_op | source)
XLA Modules:
  0.0 252.5 jit_solution(11337429251947719140)
XLA Ops:
  6.5 2.5 collective-permute-start.3
  9.1 4.4 %collective-permute-start.2 = (s32[64]{0:T(128)}, s32[64]{0:T(128)S(1)}, u32[]{:S(2)}, u32[]{:S(2)}) collective-permute-start(s32[64]{0:T(128)} %param.16), channel_id=1, source_target_pairs={{0,2},{1,3},{2,4},{3,5},{4,6},{5,7},{6,8},{7,9},{8,10},{9,11},{10,... | collective-permute-start | bytes 776 | tf_op jit(solution)/shard_map/ppermute | solution.py:28
  13.5 3.2 %collective-permute-start.1 = (bf16[64,256]{1,0:T(8,128)(2,1)S(1)}, bf16[64,256]{1,0:T(8,128)(2,1)S(1)}, u32[]{:S(2)}, u32[]{:S(2)}) collective-permute-start(bf16[64,256]{1,0:T(8,128)(2,1)S(1)} %constant_dynamic-slice_fusion.1), channel_id=1, source_target_pairs={{0,1},{1,2},{2,3},{3,4},{4,5},{5,6},{6,7},{7,8},{8,9},{9,10},{10,1... | collective-permute-start | bytes 98312 | tf_op jit(solution)/shard_map/ppermute | solution.py:28
  16.8 3.4 %collective-permute-start = (bf16[64,256]{1,0:T(8,128)(2,1)S(1)}, bf16[64,256]{1,0:T(8,128)(2,1)S(1)}, u32[]{:S(2)}, u32[]{:S(2)}) collective-permute-start(bf16[64,256]{1,0:T(8,128)(2,1)S(1)} %constant_dynamic-slice_fusion.1), channel_id=1, source_target_pairs={{0,2},{1,3},{2,4},{3,5},{4,6},{5,7},{6,8},{7,9},{8,10},{9,11},{10,... | collective-permute-start | bytes 98312 | tf_op jit(solution)/shard_map/ppermute | solution.py:28
  20.2 0.8 constant_dynamic-slice_fusion
  21.0 1.9 collective-permute-start.5
  23.8 1.5 reshape.191
  25.2 3.4 %collective-permute-start.4 = (bf16[64,256]{1,0:T(8,128)(2,1)S(1)}, bf16[64,256]{1,0:T(8,128)(2,1)S(1)}, u32[]{:S(2)}, u32[]{:S(2)}) collective-permute-start(bf16[64,256]{1,0:T(8,128)(2,1)S(1)} %constant_dynamic-slice_fusion), channel_id=1, source_target_pairs={{0,2},{1,3},{2,4},{3,5},{4,6},{5,7},{6,8},{7,9},{8,10},{9,11},{10,... | collective-permute-start | bytes 98312 | tf_op jit(solution)/shard_map/ppermute | solution.py:28
  31.9 1.1 convolution_convert_fusion.3
  33.0 1.9 copy-done.2
  34.8 3.7 %convolution_convert_fusion.2 = bf16[64,2880]{1,0:T(8,128)(2,1)S(1)} fusion(bf16[64,2048]{0,1:T(8,128)(2,1)S(1)} %bitcast.61, bf16[2048,2880]{0,1:T(8,128)(2,1)S(1)} %copy-done.2), kind=kOutput, calls=%fused_computation.11 | convolution fusion | flops 755159040 | bytes 12427264 | tf_op jit(solution)/shard_map/dot_general | solution.py:111
  38.5 12.1 %all-gather = bf16[128,2880]{1,0:T(8,128)(2,1)S(1)} all-gather(bf16[64,2880]{1,0:T(8,128)(2,1)S(1)} %convolution_convert_fusion.2), channel_id=2, replica_groups=mesh['col'=2,'row'=16] {'col'}, dimensions={0}, use_global_device_ids=true | all-gather | bytes 1105920 | tf_op jit(solution)/shard_map/all_gather | solution.py:17
  51.1 0.9 fusion.25
  52.2 20.2 %all-gather.3 = f32[16,64,8]{1,2,0:T(8,128)S(1)} all-gather(f32[1,64,8]{1,2,0:T(8,128)S(1)} %maximum_bitcast_fusion), channel_id=3, replica_groups=mesh['col'=2,'row'=16] {'row'}, dimensions={0}, use_global_device_ids=true | all-gather | bytes 34816 | tf_op jit(solution)/shard_map/all_gather | solution.py:116
  72.9 39.4 %all-gather.6.cloned.1.call-done = bf16[1024,2880]{1,0:T(8,128)(2,1)} async-done(((bf16[64,2880]{1,0:T(8,128)(2,1)}), bf16[1024,2880]{1,0:T(8,128)(2,1)}) %all-gather.6.cloned.1.call-update) | async-done | bytes 5898256 | tf_op jit(solution)/shard_map/all_gather | solution.py:131
  112.3 3.7 %convolution_convert_fusion.1 = bf16[16,32,2880]{2,1,0:T(8,128)(2,1)S(1)} fusion(bf16[16,64,2880]{2,1,0:T(8,128)(2,1)} %bitcast.55, s32[16,64]{1,0:T(8,128)S(1)} %broadcast_add_fusion, pred[16,64]{1,0:T(8,128)(4,1)S(1)} %reduce_or.9), kind=kOutput, calls=%fused_computation.10 | convolution fusion | flops 190283776 | bytes 8852480 | tf_op jit(solution)/shard_map/nst,ntd->nsd/dot_general | solution.py:133
  116.0 7.2 %fusion.2 = f32[512,1440]{0,1:T(8,128)S(1)} fusion(bf16[512,2880]{1,0:T(8,128)(2,1)S(1)} %bitcast.56, bf16[1,2,2880,1440]{2,3,1,0:T(8,128)(2,1)} %param.22), kind=kOutput, calls=%fused_computation.2 | convolution fusion | flops 4246732800 | bytes 14376960 | tf_op jit(solution)/shard_map/dot_general | solution.py:137
  123.2 8.8 %fusion.19 = bf16[512,1440]{0,1:T(8,128)(2,1)S(1)} fusion(f32[512,1440]{0,1:T(8,128)S(1)} %fusion.2, bf16[512,2880]{1,0:T(8,128)(2,1)S(1)} %bitcast.57, bf16[1,2,2880,1440]{2,3,1,0:T(8,128)(2,1)} %param.22), kind=kOutput, calls=%fused_computation.15 | convolution fusion | flops 4252631040 | bytes 15851520 | tf_op jit(solution)/shard_map/dot_general | solution.py:138
  132.7 10.8 %convolution_convert_fusion = bf16[16,64,2880]{2,1,0:T(8,128)(2,1)} fusion(bf16[16,32,1440]{2,1,0:T(8,128)(2,1)S(1)} %bitcast.60, bf16[1,1440,2880]{2,1,0:T(8,128)(2,1)} %param.23, f32[16,32]{1,0:T(8,128)S(1)} %select_reduce_fusion, s32[16,64]{1,0:T(8,128)S(1)} %broadcast_add_fusion, pred[16,64]{1,0:T(8,128)(4,1)S(1)} %reduce_or.9), kind=kOutput, calls=%fused_computation.9 | convolution fusion | flops 4441440256 | bytes 15674368 | tf_op jit(solution)/shard_map/nst,nsd->ntd/dot_general | solution.py:143
  143.6 81.9 %reduce-scatter.5.cloned.1.call-done = bf16[64,2880]{1,0:T(8,128)(2,1)} async-done(((bf16[1024,2880]{1,0:T(8,128)(2,1)}), bf16[64,2880]{1,0:T(8,128)(2,1)}) %reduce-scatter.5.cloned.1.call-update) | async-done | bytes 368656 | tf_op jit(solution)/shard_map/reduce_scatter | solution.py:152
  225.5 2.1 copy.26
  227.7 16.4 %reduce-scatter.7.cloned.1.call-done = bf16[1440,64]{1,0:T(8,128)(2,1)} async-done(((bf16[2880,64]{1,0:T(8,128)(2,1)}), bf16[1440,64]{1,0:T(8,128)(2,1)}) %reduce-scatter.7.cloned.1.call-update) | async-done | bytes 184336
  244.0 1.1 copy.27
  245.2 0.8 add_convert_fusion.1
  (52 shorter events, 5.8 us)
Async XLA Ops:
  6.5 7.0 %copy-start = (bf16[64,512]{1,0:T(8,128)(2,1)S(1)}, bf16[64,512]{1,0:T(8,128)(2,1)}, u32[]{:S(2)}) copy-start(bf16[64,512]{1,0:T(8,128)(2,1)} %param.15) | copy-start | bytes 196612
  6.5 105.8 %all-gather.6.cloned.1.call-start = ((), (), s32[]{:S(2)}) async-start(), calls=%async_computation.3 | async-start | bytes 6406144 | tf_op jit(solution)/shard_map/all_gather | solution.py:131
  6.5 18.7 %collective-permute-start.3 = (s32[64]{0:T(128)}, s32[64]{0:T(128)S(1)}, u32[]{:S(2)}, u32[]{:S(2)}) collective-permute-start(s32[64]{0:T(128)} %param.16), channel_id=1, source_target_pairs={{0,1},{1,2},{2,3},{3,4},{4,5},{5,6},{6,7},{7,8},{8,9},{9,10},{10,1... | collective-permute-start | bytes 776 | tf_op jit(solution)/shard_map/ppermute | solution.py:28
  9.1 19.6 %collective-permute-start.2 = (s32[64]{0:T(128)}, s32[64]{0:T(128)S(1)}, u32[]{:S(2)}, u32[]{:S(2)}) collective-permute-start(s32[64]{0:T(128)} %param.16), channel_id=1, source_target_pairs={{0,2},{1,3},{2,4},{3,5},{4,6},{5,7},{6,8},{7,9},{8,10},{9,11},{10,... | collective-permute-start | bytes 776 | tf_op jit(solution)/shard_map/ppermute | solution.py:28
  13.5 16.6 %collective-permute-start.1 = (bf16[64,256]{1,0:T(8,128)(2,1)S(1)}, bf16[64,256]{1,0:T(8,128)(2,1)S(1)}, u32[]{:S(2)}, u32[]{:S(2)}) collective-permute-start(bf16[64,256]{1,0:T(8,128)(2,1)S(1)} %constant_dynamic-slice_fusion.1), channel_id=1, source_target_pairs={{0,1},{1,2},{2,3},{3,4},{4,5},{5,6},{6,7},{7,8},{8,9},{9,10},{10,1... | collective-permute-start | bytes 98312 | tf_op jit(solution)/shard_map/ppermute | solution.py:28
  16.8 13.4 %collective-permute-start = (bf16[64,256]{1,0:T(8,128)(2,1)S(1)}, bf16[64,256]{1,0:T(8,128)(2,1)S(1)}, u32[]{:S(2)}, u32[]{:S(2)}) collective-permute-start(bf16[64,256]{1,0:T(8,128)(2,1)S(1)} %constant_dynamic-slice_fusion.1), channel_id=1, source_target_pairs={{0,2},{1,3},{2,4},{3,5},{4,6},{5,7},{6,8},{7,9},{8,10},{9,11},{10,... | collective-permute-start | bytes 98312 | tf_op jit(solution)/shard_map/ppermute | solution.py:28
  21.0 9.3 %collective-permute-start.5 = (bf16[64,256]{1,0:T(8,128)(2,1)S(1)}, bf16[64,256]{1,0:T(8,128)(2,1)S(1)}, u32[]{:S(2)}, u32[]{:S(2)}) collective-permute-start(bf16[64,256]{1,0:T(8,128)(2,1)S(1)} %constant_dynamic-slice_fusion), channel_id=1, source_target_pairs={{0,1},{1,2},{2,3},{3,4},{4,5},{5,6},{6,7},{7,8},{8,9},{9,10},{10,1... | collective-permute-start | bytes 98312 | tf_op jit(solution)/shard_map/ppermute | solution.py:28
  25.2 5.1 %collective-permute-start.4 = (bf16[64,256]{1,0:T(8,128)(2,1)S(1)}, bf16[64,256]{1,0:T(8,128)(2,1)S(1)}, u32[]{:S(2)}, u32[]{:S(2)}) collective-permute-start(bf16[64,256]{1,0:T(8,128)(2,1)S(1)} %constant_dynamic-slice_fusion), channel_id=1, source_target_pairs={{0,2},{1,3},{2,4},{3,5},{4,6},{5,7},{6,8},{7,9},{8,10},{9,11},{10,... | collective-permute-start | bytes 98312 | tf_op jit(solution)/shard_map/ppermute | solution.py:28
  30.5 4.4 %copy-start.2 = (bf16[2048,2880]{0,1:T(8,128)(2,1)S(1)}, bf16[2048,2880]{0,1:T(8,128)(2,1)}, u32[]{:S(2)}) copy-start(bf16[2048,2880]{0,1:T(8,128)(2,1)} %param.18) | copy-start | bytes 35389444
  34.8 16.0 %copy-start.3 = (bf16[64,2880]{1,0:T(8,128)(2,1)S(1)}, bf16[64,2880]{1,0:T(8,128)(2,1)}, u32[]{:S(2)}) copy-start(bf16[64,2880]{1,0:T(8,128)(2,1)} %param.12) | copy-start | bytes 1105924
  38.5 12.6 %copy-start.4 = (f32[2880]{0:T(1024)S(1)}, f32[2880]{0:T(1024)}, u32[]{:S(2)}) copy-start(f32[2880]{0:T(1024)} %param.19) | copy-start | bytes 34564
  38.5 13.6 %copy-start.5 = (s32[64,4]{0,1:T(4,128)S(1)}, s32[64,4]{0,1:T(4,128)}, u32[]{:S(2)}) copy-start(s32[64,4]{0,1:T(4,128)} %param.20) | copy-start | bytes 3076
  38.5 13.6 %copy-start.6 = (f32[64,4]{0,1:T(4,128)S(1)}, f32[64,4]{0,1:T(4,128)}, u32[]{:S(2)}) copy-start(f32[64,4]{0,1:T(4,128)} %param.21) | copy-start | bytes 3076
  52.1 173.5 %reduce-scatter.5.cloned.1.call-start = ((), (), s32[]{:S(2)}) async-start(), calls=%async_computation.2 | async-start | bytes 6406144 | tf_op jit(solution)/shard_map/reduce_scatter | solution.py:152
  143.5 102.5 %copy-start.1 = (bf16[64,512]{1,0:T(8,128)(2,1)S(1)}, bf16[64,512]{1,0:T(8,128)(2,1)}, u32[]{:S(2)}) copy-start(bf16[64,512]{1,0:T(8,128)(2,1)} %param.15) | copy-start | bytes 196612
  143.5 100.5 %reduce-scatter.7.cloned.1.call-start = ((), (), s32[]{:S(2)}) async-start(), calls=%async_computation.4 | async-start | bytes 1105920
Sparse Core Ops, SparseCore 0:
  52.2 60.0 all-gather.5
  143.7 81.8 reduce-scatter.4
  227.8 16.1 reduce-scatter.6
